TPU v7x, 32 devices: a whole 2x2x4 slice. The times are simulated.
32 devices in a mesh: fsdp: 32 (over z, y, x, core).
Axes of the slice: x: 2, y: 2, z: 4, core: 2. Of those that a mesh axis runs over, the one named last changes fastest.
Arguments:
- tokens: bfloat16 [4096, 1024], P('fsdp'), may hold values from -160 to 160
- seq_ids: int32 [4096], P('fsdp'), may hold values from 0 to 64, as said below
- grad_output: bfloat16 [4096, 1024], P('fsdp'), may hold values from -6 to 6
- qkv_weight: bfloat16 [3145728], P('fsdp'), may hold values from -0.1875 to 0.1875
- out_weight: bfloat16 [1048576], P('fsdp'), may hold values from -1 to 1
- up_weight: bfloat16 [4194304], P('fsdp'), may hold values from -0.1875 to 0.1875
- down_weight: bfloat16 [4194304], P('fsdp'), may hold values from -0.09375 to 0.09375
- small_params: bfloat16 [12288], P('fsdp'), may hold values from 0.5 to 1.5
Outputs:
- output: bfloat16 [4096, 1024], P('fsdp')
- tokens_grad: bfloat16 [4096, 1024], P('fsdp')
- qkv_weight_grad: float32 [3145728], P('fsdp')
- out_weight_grad: float32 [1048576], P('fsdp')
- up_weight_grad: float32 [4194304], P('fsdp')
- down_weight_grad: float32 [4194304], P('fsdp')
- small_params_grad: float32 [12288], P('fsdp')
Inputs may be any that keep to these rules, and one draw needn't show every extreme that they name: `seq_ids`: within each block of 128 rows the numbers start at 0, rise by one at the first row of each new sequence and never fall; a sequence holds 1 to 64 rows, never crosses a multiple of 64 rows, and every block holds one sequence of exactly 64 rows.
All inputs are finite; a program needn't handle non-finite values.
Results may differ from a plain program's by a relative error of at most 0.012.
The roundings to bfloat16 on the way count: a program that leaves them out, or rounds other values in their place, can miss the bound.
Values may be sent and summed in bfloat16 or wider, within the bound.
A program may use at most 256 MiB of HBM per device.

v0:
```python
import jax
import jax.numpy as jnp
from jax import lax
from jax.sharding import PartitionSpec as P

D = 1024
HEAD_DIM = 64
FF = 4096
TOK_DEV = 128
EPS = 1e-06
ROOT_HALF = 0.7071067811865476
INV_ROOT_TAU = 0.3989422804014327


def matmul(former, latter):
    return jnp.dot(former, latter, preferred_element_type=jnp.float32)


def matmul_tn(former, latter):
    return lax.dot_general(
        former, latter, (((0,), (0,)), ((), ())), preferred_element_type=jnp.float32
    )


def matmul_nt(former, latter):
    return lax.dot_general(
        former, latter, (((1,), (1,)), ((), ())), preferred_element_type=jnp.float32
    )


def unpack(params):
    params = params.astype(jnp.float32)
    bounds = [0, D, 2 * D, 3 * D, 4 * D, 5 * D, 5 * D + FF, 6 * D + FF, 7 * D + FF, 8 * D + FF]
    return [params[bounds[position] : bounds[position + 1]] for position in range(9)]


def shaped(pieces):
    return (
        pieces[0].reshape(D, 3 * D),
        pieces[1].reshape(D, D),
        pieces[2].reshape(D, FF),
        pieces[3].reshape(FF, D),
        pieces[4],
    )


def norm_forward(values, gain, shift):
    center = values - jnp.mean(values, axis=-1, keepdims=True)
    inverse = lax.rsqrt(jnp.mean(center * center, axis=-1, keepdims=True) + EPS)
    normed = center * inverse
    return (normed * gain + shift, normed, inverse)


def norm_backward(upstream, normed, inverse, gain):
    scaled = upstream * gain
    return inverse * (
        scaled
        - jnp.mean(scaled, axis=-1, keepdims=True)
        - normed * jnp.mean(scaled * normed, axis=-1, keepdims=True)
    )


def gelu_curve(values):
    return 0.5 * values * (1.0 + lax.erf(values * ROOT_HALF))


def gelu_slope(values):
    return (
        0.5 * (1.0 + lax.erf(values * ROOT_HALF))
        + values * jnp.exp(-0.5 * values * values) * INV_ROOT_TAU
    )


def split_heads(matrix):
    return matrix.reshape(-1, TOK_DEV, matrix.shape[1] // HEAD_DIM, HEAD_DIM)


def block_mask(ids):
    blocks = ids.reshape(-1, TOK_DEV)
    return (blocks[:, :, None] == blocks[:, None, :])[:, None]


def masked_scores(queries, key_rows, same_seq):
    scores = jnp.einsum(
        "bqhd,bkhd->bhqk",
        split_heads(queries),
        split_heads(key_rows),
        preferred_element_type=jnp.float32,
    ) * HEAD_DIM ** (-0.5)
    return jnp.where(same_seq, scores, -jnp.inf)


def attend(queries, key_rows, value_rows, same_seq):
    scores = masked_scores(queries, key_rows, same_seq)
    row_max = jnp.max(scores, axis=-1, keepdims=True)
    log_total = row_max + jnp.log(jnp.sum(jnp.exp(scores - row_max), axis=-1, keepdims=True))
    attn_probs = jnp.exp(scores - log_total).astype(jnp.bfloat16)
    context = (
        jnp.einsum(
            "bhqk,bkhd->bqhd",
            attn_probs,
            split_heads(value_rows),
            preferred_element_type=jnp.float32,
        )
        .reshape(-1, queries.shape[1])
        .astype(jnp.bfloat16)
    )
    return (context, log_total)


def attend_back(queries, key_rows, value_rows, same_seq, log_total, context_grad):
    columns = queries.shape[1]
    probs_full = jnp.exp(masked_scores(queries, key_rows, same_seq) - log_total)
    probs_bf = probs_full.astype(jnp.bfloat16)
    prob_grad = jnp.einsum(
        "bqhd,bkhd->bhqk",
        split_heads(context_grad),
        split_heads(value_rows),
        preferred_element_type=jnp.float32,
    )
    value_grad = jnp.einsum(
        "bhqk,bqhd->bkhd", probs_bf, split_heads(context_grad), preferred_element_type=jnp.float32
    ).reshape(-1, columns)
    row_delta = jnp.sum(probs_full * prob_grad, axis=-1, keepdims=True)
    score_grad = (probs_full * (prob_grad - row_delta) * HEAD_DIM ** (-0.5)).astype(jnp.bfloat16)
    query_grad = jnp.einsum(
        "bhqk,bkhd->bqhd", score_grad, split_heads(key_rows), preferred_element_type=jnp.float32
    ).reshape(-1, columns)
    key_grad = jnp.einsum(
        "bhqk,bqhd->bkhd", score_grad, split_heads(queries), preferred_element_type=jnp.float32
    ).reshape(-1, columns)
    return (query_grad, key_grad, value_grad)


def forward_pass(tokens, seq_ids, weights):
    qkv_matrix, out_matrix, up_matrix, down_matrix, bias_gain = weights
    (
        query_bias,
        value_bias,
        out_bias,
        gain_one,
        shift_one,
        up_bias,
        down_bias,
        gain_two,
        shift_two,
    ) = unpack(bias_gain)
    same_seq = block_mask(seq_ids)
    projected = matmul(tokens, qkv_matrix)
    queries = (projected[:, :D] + query_bias).astype(jnp.bfloat16)
    key_rows = projected[:, D : 2 * D].astype(jnp.bfloat16)
    value_rows = (projected[:, 2 * D :] + value_bias).astype(jnp.bfloat16)
    context, log_total = attend(queries, key_rows, value_rows, same_seq)
    first_sum = tokens.astype(jnp.float32) + matmul(context, out_matrix) + out_bias
    first_norm, first_unit, first_inv = norm_forward(first_sum, gain_one, shift_one)
    first_bf = first_norm.astype(jnp.bfloat16)
    hidden_pre = matmul(first_bf, up_matrix) + up_bias
    activated = gelu_curve(hidden_pre).astype(jnp.bfloat16)
    second_sum = first_norm + matmul(activated, down_matrix) + down_bias
    result, second_unit, second_inv = norm_forward(second_sum, gain_two, shift_two)
    kept = (
        same_seq,
        queries,
        key_rows,
        value_rows,
        log_total,
        context,
        first_unit,
        first_inv,
        first_bf,
        hidden_pre,
        activated,
        second_unit,
        second_inv,
    )
    return (result.astype(jnp.bfloat16), kept)


def mlp_backward(grad_output, kept, weights):
    qkv_matrix, out_matrix, up_matrix, down_matrix, bias_gain = weights
    gain_two = unpack(bias_gain)[7]
    first_bf, hidden_pre, activated, second_unit, second_inv = (
        kept[8],
        kept[9],
        kept[10],
        kept[11],
        kept[12],
    )
    out_cot = grad_output.astype(jnp.float32)
    gain_two_grad = jnp.sum(out_cot * second_unit, axis=0)
    shift_two_grad = jnp.sum(out_cot, axis=0)
    second_grad = norm_backward(out_cot, second_unit, second_inv, gain_two)
    down_bias_grad = jnp.sum(second_grad, axis=0)
    second_bf = second_grad.astype(jnp.bfloat16)
    down_grad = matmul_tn(activated, second_bf)
    hidden_grad = matmul_nt(second_bf, down_matrix) * gelu_slope(hidden_pre)
    up_bias_grad = jnp.sum(hidden_grad, axis=0)
    hidden_bf = hidden_grad.astype(jnp.bfloat16)
    up_grad = matmul_tn(first_bf, hidden_bf)
    first_grad = second_grad + matmul_nt(hidden_bf, up_matrix)
    return (
        first_grad,
        up_grad,
        down_grad,
        (up_bias_grad, down_bias_grad, gain_two_grad, shift_two_grad),
    )


def attention_backward(tokens, first_grad, kept, weights):
    qkv_matrix, out_matrix, up_matrix, down_matrix, bias_gain = weights
    gain_one = unpack(bias_gain)[3]
    same_seq, queries, key_rows, value_rows, log_total, context, first_unit, first_inv = kept[:8]
    gain_one_grad = jnp.sum(first_grad * first_unit, axis=0)
    shift_one_grad = jnp.sum(first_grad, axis=0)
    residual_grad = norm_backward(first_grad, first_unit, first_inv, gain_one)
    out_bias_grad = jnp.sum(residual_grad, axis=0)
    residual_bf = residual_grad.astype(jnp.bfloat16)
    out_grad = matmul_tn(context, residual_bf)
    context_grad = matmul_nt(residual_bf, out_matrix).astype(jnp.bfloat16)
    query_grad, key_grad, value_grad = attend_back(
        queries, key_rows, value_rows, same_seq, log_total, context_grad
    )
    query_bias_grad = jnp.sum(query_grad, axis=0)
    value_bias_grad = jnp.sum(value_grad, axis=0)
    joined_bf = jnp.concatenate([query_grad, key_grad, value_grad], axis=1).astype(jnp.bfloat16)
    qkv_grad = matmul_tn(tokens, joined_bf)
    tokens_grad = (residual_grad + matmul_nt(joined_bf, qkv_matrix)).astype(jnp.bfloat16)
    return (
        tokens_grad,
        qkv_grad,
        out_grad,
        (query_bias_grad, value_bias_grad, out_bias_grad, gain_one_grad, shift_one_grad),
    )


def shards(
    tokens, seq_ids, grad_output, qkv_weight, out_weight, up_weight, down_weight, small_params
):
    gathered = (
        lax.all_gather(qkv_weight, "fsdp", axis=0, tiled=True),
        lax.all_gather(out_weight, "fsdp", axis=0, tiled=True),
        lax.all_gather(up_weight, "fsdp", axis=0, tiled=True),
        lax.all_gather(down_weight, "fsdp", axis=0, tiled=True),
        lax.all_gather(small_params, "fsdp", axis=0, tiled=True),
    )
    result, kept = forward_pass(tokens, seq_ids, shaped(gathered))
    regained = (
        lax.all_gather(qkv_weight, "fsdp", axis=0, tiled=True),
        lax.all_gather(out_weight, "fsdp", axis=0, tiled=True),
        lax.all_gather(up_weight, "fsdp", axis=0, tiled=True),
        lax.all_gather(down_weight, "fsdp", axis=0, tiled=True),
        lax.all_gather(small_params, "fsdp", axis=0, tiled=True),
    )
    weights = shaped(regained)
    first_grad, up_grad, down_grad, mlp_small = mlp_backward(grad_output, kept, weights)
    tokens_grad, qkv_grad, out_grad, attn_small = attention_backward(
        tokens, first_grad, kept, weights
    )
    small_grad = jnp.concatenate(list(attn_small) + list(mlp_small))
    qkv_share, out_share, up_share, down_share, small_share = (
        lax.psum_scatter(qkv_grad.reshape(-1), "fsdp", scatter_dimension=0, tiled=True),
        lax.psum_scatter(out_grad.reshape(-1), "fsdp", scatter_dimension=0, tiled=True),
        lax.psum_scatter(up_grad.reshape(-1), "fsdp", scatter_dimension=0, tiled=True),
        lax.psum_scatter(down_grad.reshape(-1), "fsdp", scatter_dimension=0, tiled=True),
        lax.psum_scatter(small_grad, "fsdp", scatter_dimension=0, tiled=True),
    )
    return (result, tokens_grad, qkv_share, out_share, up_share, down_share, small_share)


def solution(mesh):
    in_specs = (
        P("fsdp", None),
        P("fsdp"),
        P("fsdp", None),
        P("fsdp"),
        P("fsdp"),
        P("fsdp"),
        P("fsdp"),
        P("fsdp"),
    )
    out_specs = (
        P("fsdp", None),
        P("fsdp", None),
        P("fsdp"),
        P("fsdp"),
        P("fsdp"),
        P("fsdp"),
        P("fsdp"),
    )
    return jax.shard_map(shards, mesh=mesh, in_specs=in_specs, out_specs=out_specs, check_vma=False)
```

profile of v0, /device:TPU:0, one launch (start us, length us, event | category | flops | bytes accessed | tf_op | source)
XLA Modules:
  0.0 1156.3 jit_solution(16009765625532053074)
XLA Ops:
  10.7 43.4 %all-gather = bf16[32,1,384]{2,1,0:T(2,128)(2,1)S(1)} all-gather(bf16[1,1,384]{2,1,0:T(2,128)(2,1)S(1)} %reshape.250), channel_id=1, replica_groups=mesh['fsdp'=32] {'fsdp'}, dimensions={0}, use_global_device_ids=true | all-gather | bytes 25344 | tf_op jit(solution)/shard_map/all_gather | solution.py:244
  55.0 14.9 %all-gather.8.cloned.1.call-done = bf16[1048576]{0:T(1024)(128)(2,1)} async-done(((bf16[32768]{0:T(1024)(128)(2,1)}), bf16[1048576]{0:T(1024)(128)(2,1)}) %all-gather.8.cloned.1.call-update) | async-done | bytes 2097168 | tf_op jit(solution)/shard_map/all_gather | solution.py:241
  69.8 2.8 reshape.239
  72.7 68.1 %all-gather.6.cloned.1.call-done = bf16[3145728]{0:T(1024)(128)(2,1)} async-done(((bf16[98304]{0:T(1024)(128)(2,1)}), bf16[3145728]{0:T(1024)(128)(2,1)}) %all-gather.6.cloned.1.call-update) | async-done | bytes 6291472 | tf_op jit(solution)/shard_map/all_gather | solution.py:240
  140.7 10.3 reshape.235
  151.0 3.8 fusion.63
  157.2 62.0 %all-gather.10.cloned.1.call-done = bf16[4194304]{0:T(1024)(128)(2,1)} async-done(((bf16[131072]{0:T(1024)(128)(2,1)}), bf16[4194304]{0:T(1024)(128)(2,1)}) %all-gather.10.cloned.1.call-update) | async-done | bytes 8388624 | tf_op jit(solution)/shard_map/all_gather | solution.py:242
  219.2 13.4 %reshape.240 = bf16[1024,4096]{1,0:T(8,128)(2,1)} reshape(bf16[4194304]{0:T(1024)(128)(2,1)} %all-gather.10.cloned.1.call-done) | data formatting | bytes 16777216 | tf_op jit(solution)/shard_map/reshape | solution.py:41
  232.6 4.8 convolution_add_fusion
  237.3 60.3 %all-gather.12.cloned.1.call-done = bf16[4194304]{0:T(1024)(128)(2,1)} async-done(((bf16[131072]{0:T(1024)(128)(2,1)}), bf16[4194304]{0:T(1024)(128)(2,1)}) %all-gather.12.cloned.1.call-update) | async-done | bytes 8388624 | tf_op jit(solution)/shard_map/all_gather | solution.py:243
  297.6 13.3 %reshape.241 = bf16[4096,1024]{1,0:T(8,128)(2,1)} reshape(bf16[4194304]{0:T(1024)(128)(2,1)} %all-gather.12.cloned.1.call-done) | data formatting | bytes 16777216 | tf_op jit(solution)/shard_map/reshape | solution.py:42
  310.9 5.0 fusion.59
  317.4 3.5 fusion.62
  321.0 3.0 multiply_reduce_fusion.1
  328.4 2.5 fusion.54
  330.9 2.4 fusion.64
  333.2 3.7 convolution_convert_fusion
  336.9 3.7 fusion.55
  340.6 1.8 convolution_bitcast_fusion.3
  342.4 8.1 convolution_bitcast_fusion
  350.5 8.2 convolution_bitcast_fusion.1
  358.7 3.0 copy.50
  361.7 6.5 convolution_bitcast_fusion.2
  368.2 12.6 %copy.44 = f32[1024,3072]{1,0:T(8,128)} copy(f32[1024,3072]{0,1:T(8,128)} %convolution_bitcast_fusion.2) | data formatting | bytes 25165824 | tf_op jit(solution)/shard_map/dot_general | solution.py:20
  380.7 12.0 %copy.49 = f32[128,24,8,128]{3,1,2,0:T(8,128)} copy(f32[128,24,8,128]{3,2,1,0:T(8,128)} %bitcast.66) | data formatting | bytes 25165824
  392.8 14.1 %copy.52 = f32[512,8,8,128]{3,1,2,0:T(8,128)} copy(f32[512,8,8,128]{3,2,1,0:T(8,128)} %convolution_bitcast_fusion) | data formatting | bytes 33554432
  406.9 14.1 %copy.51 = f32[128,32,8,128]{3,1,2,0:T(8,128)} copy(f32[128,32,8,128]{3,2,1,0:T(8,128)} %convolution_bitcast_fusion.1) | data formatting | bytes 33554432
  421.2 41.5 %all-reduce.4 = f32[12288]{0:T(1024)S(1)} all-reduce(f32[12288]{0:T(1024)S(1)} %constant_dynamic-update-slice_fusion), channel_id=6, replica_groups=mesh['fsdp'=32] {'fsdp'}, use_global_device_ids=true, to_apply=%region_24.25.clone | all-reduce | flops 12288 | bytes 98304
  463.4 5.9 fusion.12
  469.3 673.4 %all-reduce.8.cloned.1.call-done = (f32[3145728]{0:T(1024)}, f32[1048576]{0:T(1024)}, f32[4194304]{0:T(1024)}, f32[4194304]{0:T(1024)}) async-done(((f32[3145728]{0:T(1024)}, f32[1048576]{0:T(1024)}, f32[4194304]{0:T(1024)}, f32[4194304]{0:T(1024)}), (f32[3145728]{0:T(1024)}, f32[1048576]{0:T(1024)}, f32[4194304]{0:T(1024)}, f32[4194304]{0:T(1024)})) %all-reduce.8.cloned.1.call-update) | async-done | bytes 50331664
  1142.7 1.9 dynamic-slice.2
  1144.5 1.9 dynamic-slice.3
  (95 shorter events, 16.6 us)
Async XLA Ops:
  7.2 62.6 %all-gather.8.cloned.1.call-start = ((), (), s32[]{:S(2)}) async-start(), calls=%async_computation.1 | async-start | bytes 2162688 | tf_op jit(solution)/shard_map/all_gather | solution.py:241
  7.9 132.8 %all-gather.6.cloned.1.call-start = ((), (), s32[]{:S(2)}) async-start(), calls=%async_computation | async-start | bytes 6488064 | tf_op jit(solution)/shard_map/all_gather | solution.py:240
  8.6 210.5 %all-gather.10.cloned.1.call-start = ((), (), s32[]{:S(2)}) async-start(), calls=%async_computation.2 | async-start | bytes 8650752 | tf_op jit(solution)/shard_map/all_gather | solution.py:242
  9.4 288.2 %all-gather.12.cloned.1.call-start = ((), (), s32[]{:S(2)}) async-start(), calls=%async_computation.3 | async-start | bytes 8650752 | tf_op jit(solution)/shard_map/all_gather | solution.py:243
  10.0 1132.7 %all-reduce.8.cloned.1.call-start = ((), (), s32[]{:S(2)}) async-start(), calls=%async_computation.4 | async-start | bytes 100663296
  72.6 83.8 %copy-start = (bf16[1024,1024]{1,0:T(8,128)(2,1)}, bf16[1024,1024]{1,0:T(8,128)(2,1)S(1)}, u32[]{:S(2)}) copy-start(bf16[1024,1024]{1,0:T(8,128)(2,1)S(1)} %reshape.239) | copy-start | bytes 6291460
  72.6 78.4 %copy-start.7 = (bf16[128,1024]{1,0:T(8,128)(2,1)S(1)}, bf16[128,1024]{1,0:T(8,128)(2,1)}, u32[]{:S(2)}) copy-start(bf16[128,1024]{1,0:T(8,128)(2,1)} %param.8) | copy-start | bytes 786436
  155.2 0.9 copy-start.13
  155.4 1.1 copy-start.12
  155.5 0.9 copy-start.8
  155.9 1.1 copy-start.2
  156.4 76.1 %copy-start.9 = (bf16[16,64,128]{2,1,0:T(8,128)(2,1)}, bf16[16,64,128]{2,1,0:T(8,128)(2,1)S(1)}, u32[]{:S(2)}) copy-start(bf16[16,64,128]{2,1,0:T(8,128)(2,1)S(1)} %convolution_convert_fusion.2) | copy-start | bytes 786436
  310.9 6.5 slice-start.2
  310.9 5.3 copy-start.11
  310.9 6.5 slice-start.3
  316.5 4.5 slice-start
  317.4 3.5 slice-start.1
  320.9 3.1 copy-start.5
  320.9 4.1 copy-start.1
  324.2 0.8 copy-start.3
  342.4 8.1 copy-start.6
  358.7 3.0 copy-start.10
  358.7 3.0 copy-start.14
  358.7 3.0 copy-start.15
  421.0 42.4 %copy-start.4 = (f32[128,1024]{1,0:T(8,128)S(1)}, f32[128,1024]{1,0:T(8,128)}, u32[]{:S(2)}) copy-start(f32[128,1024]{1,0:T(8,128)} %copy-done.3) | copy-start | bytes 1572868
Sparse Core Ops, SparseCore 0:
  10.8 58.9 all-gather.7
  72.7 67.9 all-gather.5
  143.6 75.5 all-gather.9
  221.9 75.6 all-gather.11
  421.1 721.5 all-reduce.7
where the time goes:
time: 1160 us
  waiting for transfers between devices  881 us (76%)
  local copies, waits for them, and re-layouts  107 us (9%)
  blocking collectives  84.9 us (7%)
  matrix products  65.5 us (6%)
  between operations  14.2 us (1%)
    unnamed x6, waiting for transfers between devices  676 us
    all_gather x1, waiting for transfers between devices, shards(): lax.all_gather(qkv_weight, 'fsdp', axis=0, tiled=True)  68.1 us
    all_gather x1, waiting for transfers between devices, shards(): lax.all_gather(up_weight, 'fsdp', axis=0, tiled=True)  62 us
    all_gather x1, waiting for transfers between devices, shards(): lax.all_gather(down_weight, 'fsdp', axis=0, tiled=True)  60.3 us
    unnamed x58, local copies, waits for them, and re-layouts  52.5 us
    all_gather x1, blocking collectives, shards(): lax.all_gather(small_params, 'fsdp', axis=0, tiled=True)  43.4 us
    unnamed x1, blocking collectives  41.5 us
    dot_general x4, matrix products, matmul_tn(): lax.dot_general(former, latter, (((0,), (0,)), ((), ())), preferred_eleme...  24.6 us
  transfers between devices with their start and end apart: 5, of which 5 were waited for; matrix products, arithmetic and copies ran while one was open for 4% of the time, Pallas kernels for 0%

commit v1 on v0

--- a/solution.py
+++ b/solution.py
@@ -10,6 +10,18 @@
 EPS = 1e-06
 ROOT_HALF = 0.7071067811865476
 INV_ROOT_TAU = 0.3989422804014327
+
+
+def collect(shard, axis, dim):
+    ways, here, hop = (lax.axis_size(axis), lax.axis_index(axis), shard.shape[dim])
+    line, have = (shard, 1)
+    while have < ways:
+        line = jnp.concatenate(
+            [line, lax.ppermute(line, axis, [(d, (d - have) % ways) for d in range(ways)])],
+            axis=dim,
+        )
+        have = 2 * have
+    return jnp.roll(line, here * hop, axis=dim)
 
 
 def matmul(former, latter):
@@ -240,7 +252,7 @@
         lax.all_gather(qkv_weight, "fsdp", axis=0, tiled=True),
         lax.all_gather(out_weight, "fsdp", axis=0, tiled=True),
         lax.all_gather(up_weight, "fsdp", axis=0, tiled=True),
-        lax.all_gather(down_weight, "fsdp", axis=0, tiled=True),
+        collect(down_weight, "fsdp", 0),
         lax.all_gather(small_params, "fsdp", axis=0, tiled=True),
     )
     result, kept = forward_pass(tokens, seq_ids, shaped(gathered))

time: 1160 us -> 1390 us (1.20)
  blocking collectives: 84.9 us -> 170 us
  waiting for transfers between devices: 881 us -> 966 us
  local copies, waits for them, and re-layouts: 107 us -> 148 us
  starting transfers between devices: 0.19 us -> 14.3 us
    ppermute x0 -> x5, waiting for transfers between devices: none -> 135 us  [collect(): lax.ppermute(line, axis, [(d, (d - have) % ways) for d in range(ways)])]
    all_gather x1, blocking collectives: 43.4 us -> 129 us  [shards(): lax.all_gather(small_params, 'fsdp', axis=0, tiled=True)]
    all_gather x1, waiting for transfers between devices: 68.1 us -> 39.8 us  [shards(): lax.all_gather(qkv_weight, 'fsdp', axis=0, tiled=True)]
    all_gather x1, waiting for transfers between devices: 14.9 us -> 0.02 us  [shards(): lax.all_gather(out_weight, 'fsdp', axis=0, tiled=True)]
    unnamed x58 -> x80, local copies, waits for them, and re-layouts: 52.5 us -> 66.9 us
    ppermute x0 -> x5, starting transfers between devices: none -> 14.1 us  [collect(): lax.ppermute(line, axis, [(d, (d - have) % ways) for d in range(ways)])]
  transfers between devices with their start and end apart: 5 -> 10, of which waited for: 5 -> 9; matrix products, arithmetic and copies ran while one was open for 4% -> 7% of each run, Pallas kernels for 0% -> 0%
where the time goes in v1:
time: 1390 us
  waiting for transfers between devices  966 us (69%)
  blocking collectives  170 us (12%)
  local copies, waits for them, and re-layouts  148 us (11%)
  matrix products  72.3 us (5%)
  starting transfers between devices  14.3 us (1%)
  between operations  14.3 us (1%)
    unnamed x6, waiting for transfers between devices  675 us
    ppermute x5, waiting for transfers between devices, collect(): lax.ppermute(line, axis, [(d, (d - have) % ways) for d in range(ways)])  135 us
    all_gather x1, blocking collectives, shards(): lax.all_gather(small_params, 'fsdp', axis=0, tiled=True)  129 us
    unnamed x80, local copies, waits for them, and re-layouts  66.9 us
    all_gather x1, waiting for transfers between devices, shards(): lax.all_gather(up_weight, 'fsdp', axis=0, tiled=True)  62 us
    all_gather x1, waiting for transfers between devices, shards(): lax.all_gather(down_weight, 'fsdp', axis=0, tiled=True)  53.8 us
    unnamed x1, blocking collectives  41.7 us
    all_gather x1, waiting for transfers between devices, shards(): lax.all_gather(qkv_weight, 'fsdp', axis=0, tiled=True)  39.8 us
  transfers between devices with their start and end apart: 10, of which 9 were waited for; matrix products, arithmetic and copies ran while one was open for 7% of the time, Pallas kernels for 0%

profile of v1, /device:TPU:0, one launch (start us, length us, event | category | flops | bytes accessed | tf_op | source)
XLA Modules:
  0.0 1389.7 jit_solution(3934887615424369426)
XLA Ops:
  8.7 6.5 collective-permute-start
  21.9 10.3 collective-permute-done.1
  35.4 23.2 %collective-permute-done.2 = bf16[524288]{0:T(1024)(128)(2,1)S(1)} collective-permute-done((bf16[524288]{0:T(1024)(128)(2,1)S(1)}, bf16[524288]{0:T(1024)(128)(2,1)S(1)}, u32[]{:S(2)}, u32[]{:S(2)}) %collective-permute-start.2) | collective-permute-done | bytes 1048608 | tf_op jit(solution)/shard_map/ppermute | solution.py:20
  58.8 4.5 collective-permute-start.3
  64.8 43.9 %collective-permute-done.3 = bf16[1048576]{0:T(1024)(128)(2,1)S(1)} collective-permute-done((bf16[1048576]{0:T(1024)(128)(2,1)S(1)}, bf16[1048576]{0:T(1024)(128)(2,1)S(1)}, u32[]{:S(2)}, u32[]{:S(2)}) %collective-permute-start.3) | collective-permute-done | bytes 2097184 | tf_op jit(solution)/shard_map/ppermute | solution.py:20
  113.9 128.6 %all-gather = bf16[32,1,384]{2,1,0:T(2,128)(2,1)S(1)} all-gather(bf16[1,1,384]{2,1,0:T(2,128)(2,1)S(1)} %reshape.253), channel_id=1, replica_groups=mesh['fsdp'=32] {'fsdp'}, dimensions={0}, use_global_device_ids=true | all-gather | bytes 25344 | tf_op jit(solution)/shard_map/all_gather | solution.py:256
  245.6 55.6 %collective-permute-done.4 = bf16[2097152]{0:T(1024)(128)(2,1)} collective-permute-done((bf16[2097152]{0:T(1024)(128)(2,1)}, bf16[2097152]{0:T(1024)(128)(2,1)}, u32[]{:S(2)}, u32[]{:S(2)}) %collective-permute-start.4) | collective-permute-done | bytes 4194336 | tf_op jit(solution)/shard_map/ppermute | solution.py:20
  301.2 3.8 constant_dynamic-update-slice_fusion.17
  309.8 3.7 constant_dynamic-update-slice_fusion.11
  313.5 7.1 dynamic_slice.4
  320.6 13.4 reshape.243
  333.9 39.8 %all-gather.6.cloned.1.call-done = bf16[3145728]{0:T(1024)(128)(2,1)} async-done(((bf16[98304]{0:T(1024)(128)(2,1)}), bf16[3145728]{0:T(1024)(128)(2,1)}) %all-gather.6.cloned.1.call-update) | async-done | bytes 6291472 | tf_op jit(solution)/shard_map/all_gather | solution.py:252
  373.8 10.3 reshape.237
  384.1 3.8 fusion.63
  390.3 62.0 %all-gather.10.cloned.1.call-done = bf16[4194304]{0:T(1024)(128)(2,1)} async-done(((bf16[131072]{0:T(1024)(128)(2,1)}), bf16[4194304]{0:T(1024)(128)(2,1)}) %all-gather.10.cloned.1.call-update) | async-done | bytes 8388624 | tf_op jit(solution)/shard_map/all_gather | solution.py:254
  452.3 13.4 reshape.242
  465.6 4.8 convolution_add_fusion
  470.4 5.0 fusion.59
  476.9 53.8 %all-gather.12.cloned.1.call-done = bf16[4194304]{0:T(1024)(128)(2,1)} async-done(((bf16[131072]{0:T(1024)(128)(2,1)}), bf16[4194304]{0:T(1024)(128)(2,1)}) %all-gather.12.cloned.1.call-update) | async-done | bytes 8388624 | tf_op jit(solution)/shard_map/all_gather | solution.py:263
  530.7 13.3 reshape.244
  544.0 6.5 fusion.62
  550.5 6.8 multiply_reduce_fusion.1
  575.8 8.1 convolution_bitcast_fusion
  583.9 8.4 convolution_bitcast_fusion.1
  595.3 6.3 convolution_bitcast_fusion.2
  601.6 12.6 copy.44
  614.2 12.0 copy.49
  626.2 14.1 %copy.52 = f32[512,8,8,128]{3,1,2,0:T(8,128)} copy(f32[512,8,8,128]{3,2,1,0:T(8,128)} %convolution_bitcast_fusion) | data formatting | bytes 33554432
  640.3 14.1 %copy.51 = f32[128,32,8,128]{3,1,2,0:T(8,128)} copy(f32[128,32,8,128]{3,2,1,0:T(8,128)} %convolution_bitcast_fusion.1) | data formatting | bytes 33554432
  654.6 41.7 %all-reduce.4 = f32[12288]{0:T(1024)S(1)} all-reduce(f32[12288]{0:T(1024)S(1)} %constant_dynamic-update-slice_fusion.18), channel_id=6, replica_groups=mesh['fsdp'=32] {'fsdp'}, use_global_device_ids=true, to_apply=%region_24.25.clone | all-reduce | flops 12288 | bytes 98304
  697.0 5.9 fusion.12
  703.0 673.2 %all-reduce.8.cloned.1.call-done = (f32[3145728]{0:T(1024)}, f32[1048576]{0:T(1024)}, f32[4194304]{0:T(1024)}, f32[4194304]{0:T(1024)}) async-done(((f32[3145728]{0:T(1024)}, f32[1048576]{0:T(1024)}, f32[4194304]{0:T(1024)}, f32[4194304]{0:T(1024)}), (f32[3145728]{0:T(1024)}, f32[1048576]{0:T(1024)}, f32[4194304]{0:T(1024)}, f32[4194304]{0:T(1024)})) %all-reduce.8.cloned.1.call-update) | async-done | bytes 50331664
  (132 shorter events, 59.1 us)
Async XLA Ops:
  7.2 51.5 %copy-start.3 = (bf16[131072]{0:T(1024)(128)(2,1)S(1)}, bf16[131072]{0:T(1024)(128)(2,1)}, u32[]{:S(2)}) copy-start(bf16[131072]{0:T(1024)(128)(2,1)} %param.14) | copy-start | bytes 786436
  7.2 235.5 %all-gather.8.cloned.1.call-start = ((), (), s32[]{:S(2)}) async-start(), calls=%async_computation.1 | async-start | bytes 2162688 | tf_op jit(solution)/shard_map/all_gather | solution.py:253
  7.9 365.9 %all-gather.6.cloned.1.call-start = ((), (), s32[]{:S(2)}) async-start(), calls=%async_computation | async-start | bytes 6488064 | tf_op jit(solution)/shard_map/all_gather | solution.py:252
  8.7 443.6 %all-gather.10.cloned.1.call-start = ((), (), s32[]{:S(2)}) async-start(), calls=%async_computation.2 | async-start | bytes 8650752 | tf_op jit(solution)/shard_map/all_gather | solution.py:254
  8.7 10.7 collective-permute-start
  15.2 515.5 %all-gather.12.cloned.1.call-start = ((), (), s32[]{:S(2)}) async-start(), calls=%async_computation.3 | async-start | bytes 8650752 | tf_op jit(solution)/shard_map/all_gather | solution.py:263
  19.4 39.5 %copy-start.9 = (bf16[131072]{0:T(1024)(128)(2,1)}, bf16[131072]{0:T(1024)(128)(2,1)S(1)}, u32[]{:S(2)}) copy-start(bf16[131072]{0:T(1024)(128)(2,1)S(1)} %collective-permute-done) | copy-start | bytes 786436
  20.4 11.7 collective-permute-start.1
  32.2 26.5 %copy-start.7 = (bf16[262144]{0:T(1024)(128)(2,1)}, bf16[262144]{0:T(1024)(128)(2,1)S(1)}, u32[]{:S(2)}) copy-start(bf16[262144]{0:T(1024)(128)(2,1)S(1)} %collective-permute-done.1) | copy-start | bytes 1572868
  33.4 25.3 %collective-permute-start.2 = (bf16[524288]{0:T(1024)(128)(2,1)S(1)}, bf16[524288]{0:T(1024)(128)(2,1)S(1)}, u32[]{:S(2)}, u32[]{:S(2)}) collective-permute-start(bf16[524288]{0:T(1024)(128)(2,1)S(1)} %pad_maximum_fusion.1), channel_id=1, source_target_pairs={{0,28},{1,29},{2,30},{3,31},{4,0},{5,1},{6,2},{7,3},{8,4},{9,5},{1... | collective-permute-start | bytes 3145736 | tf_op jit(solution)/shard_map/ppermute | solution.py:20
  58.8 49.9 %collective-permute-start.3 = (bf16[1048576]{0:T(1024)(128)(2,1)S(1)}, bf16[1048576]{0:T(1024)(128)(2,1)S(1)}, u32[]{:S(2)}, u32[]{:S(2)}) collective-permute-start(bf16[1048576]{0:T(1024)(128)(2,1)S(1)} %pad_maximum_fusion), channel_id=1, source_target_pairs={{0,24},{1,25},{2,26},{3,27},{4,28},{5,29},{6,30},{7,31},{8,0},{9,1... | collective-permute-start | bytes 6291464 | tf_op jit(solution)/shard_map/ppermute | solution.py:20
  63.3 50.5 %copy-start.25 = (bf16[384]{0:T(512)(128)(2,1)S(1)}, bf16[384]{0:T(512)(128)(2,1)}, u32[]{:S(2)}) copy-start(bf16[384]{0:T(512)(128)(2,1)} %param.15) | copy-start | bytes 2308
  63.3 179.2 %copy-start.24 = (s32[128]{0:T(128)S(1)}, s32[128]{0:T(128)}, u32[]{:S(2)}) copy-start(s32[128]{0:T(128)} %param.9) | copy-start | bytes 1540
  108.7 1.3 copy-start.5
  112.3 188.9 %collective-permute-start.4 = (bf16[2097152]{0:T(1024)(128)(2,1)}, bf16[2097152]{0:T(1024)(128)(2,1)}, u32[]{:S(2)}, u32[]{:S(2)}) collective-permute-start(bf16[2097152]{0:T(1024)(128)(2,1)} %get-tuple-element.23), channel_id=1, source_target_pairs={{0,16},{1,17},{2,18},{3,19},{4,20},{5,21},{6,22},{7,23},{8,24},{9,... | collective-permute-start | bytes 12582920 | tf_op jit(solution)/shard_map/ppermute | solution.py:20
  113.8 1262.3 %all-reduce.8.cloned.1.call-start = ((), (), s32[]{:S(2)}) async-start(), calls=%async_computation.4 | async-start | bytes 100663296
  245.5 144.0 %copy-start = (bf16[1024,1024]{1,0:T(8,128)(2,1)}, bf16[1024,1024]{1,0:T(8,128)(2,1)S(1)}, u32[]{:S(2)}) copy-start(bf16[1024,1024]{1,0:T(8,128)(2,1)S(1)} %reshape.241) | copy-start | bytes 6291460
  301.1 3.8 copy-start.4
  301.2 4.5 copy-start.10
  301.2 5.2 copy-start.8
  304.9 3.4 copy-start.6
  333.9 50.2 %copy-start.15 = (bf16[128,1024]{1,0:T(8,128)(2,1)S(1)}, bf16[128,1024]{1,0:T(8,128)(2,1)}, u32[]{:S(2)}) copy-start(bf16[128,1024]{1,0:T(8,128)(2,1)} %param.8) | copy-start | bytes 786436
  389.0 1.1 copy-start.2
  389.5 76.1 %copy-start.17 = (bf16[16,64,128]{2,1,0:T(8,128)(2,1)}, bf16[16,64,128]{2,1,0:T(8,128)(2,1)S(1)}, u32[]{:S(2)}) copy-start(bf16[16,64,128]{2,1,0:T(8,128)(2,1)S(1)} %convolution_convert_fusion.2) | copy-start | bytes 786436
  470.4 5.2 copy-start.19
  550.5 6.9 copy-start.13
  550.5 7.9 copy-start.1
  575.8 8.1 copy-start.14
  592.3 3.0 copy-start.18
  592.3 3.0 copy-start.22
  592.3 3.0 copy-start.23
  654.4 42.6 %copy-start.12 = (f32[128,1024]{1,0:T(8,128)S(1)}, f32[128,1024]{1,0:T(8,128)}, u32[]{:S(2)}) copy-start(f32[128,1024]{1,0:T(8,128)} %copy-done.11) | copy-start | bytes 1572868
  (4 other events, 3.7 us)
Sparse Core Ops, SparseCore 0:
  10.8 207.0 all-gather.7
  220.8 152.9 all-gather.5
  376.7 75.5 all-gather.9
  455.0 75.6 all-gather.11
  654.6 721.5 all-reduce.7
